TPU v7x, 32 devices: a whole 2x2x4 slice. The times are simulated.
32 devices in a mesh: grp: 2 (over y), seq: 4 (over z), usr: 4 (over x, core).
Axes of the slice: x: 2, y: 2, z: 4, core: 2. Of those that a mesh axis runs over, the one named last changes fastest.
Arguments:
- history_kv: bfloat16 [16, 2048, 768], P(('grp', 'usr'), 'seq'), parts along dimension 0, may hold values from -6 to 6
- candidates: bfloat16 [16, 512, 768], P(('grp', 'usr'), 'seq'), parts along dimension 0, may hold values from -6 to 6
- lengths: int32 [16], P(('grp', 'usr')), parts along dimension 0, may hold values from 256 to 2048, as said below
- w_query: bfloat16 [768, 384], replicated, may hold values from -0.21875 to 0.21875
- w_gate: bfloat16 [768, 384], replicated, may hold values from -0.21875 to 0.21875
- token_mix: bfloat16 [512, 512], P('seq'), may hold values from -0.25 to 0.25
- w_out: bfloat16 [384, 768], replicated, may hold values from -0.3125 to 0.3125
- w_up: bfloat16 [768, 2048], P(None, 'usr'), may hold values from -0.21875 to 0.21875
- w_down: bfloat16 [2048, 768], P('usr'), may hold values from -0.125 to 0.125
Outputs:
- ranked: bfloat16 [16, 512, 768], P(('grp', 'usr'), 'seq'), parts along dimension 0
There are 2 independent parts, one for each index of `grp`. A program takes and returns all parts, laid end to end along the dimension named above; an argument that names none is the same for every part. Nothing has to cross between parts.
Inputs may be any that keep to these rules, and one draw needn't show every extreme that they name: lengths[u] counts the first valid slots of user u's history; in every draw one user has exactly 2048 and another exactly 256.
All inputs are finite; a program needn't handle non-finite values.
Results may differ from a plain program's by a relative error of at most 0.008.
Values may be sent and summed in bfloat16 or wider, within the bound.
A program may use at most 64 MiB of HBM per device.

v0:
```python
import functools
import math

import jax
import jax.numpy as jnp
from jax import lax
from jax.experimental import pallas as pl
from jax.experimental.pallas import tpu as pltpu
from jax.sharding import PartitionSpec as P

HEADS = 3
DH = 128
F32 = jnp.float32
BF16 = jnp.bfloat16
MESH = pl.DeviceIdType.MESH
ACROSS_STEPS = (1, 2, 3, 4)
GROUP_STEPS = (3, 4, 5, 6)
MIX_STEP = 0
SHARE_STEPS = (3, 4)


def layer_norm(values):
    center = values - jnp.mean(values, axis=-1, keepdims=True)
    spread = jnp.mean(center * center, axis=-1, keepdims=True)
    return center * lax.rsqrt(spread + 1e-05)


def silu_of_double(half):
    return half + half * jnp.tanh(half)


def gelu_tanh(v):
    return 0.5 * v * (1.0 + jnp.tanh(math.sqrt(2.0 / math.pi) * (v + 0.044715 * (v * v * v))))


def dot(a, b):
    return jnp.dot(a, b, preferred_element_type=F32)


def kernel(
    seqs,
    kv_hbm, cand_hbm, len_ref, wq_hbm, wg_hbm, tm_hbm, wo_hbm, wu_hbm, wd_hbm,
    out_ref,
    kv, cand, wq, wg, tm, wo, wu, wd,
    values, queries, sums, outgoing, incoming, normed, mixed_out, mixed_in, gates, states,
    load_sem,
    q_send, q_recv, p_send, p_recv, t_send, t_recv, f_send, m_send, m_recv,
    wo_send, wo_recv, wc_send, wc_recv, wx_send, wx_recv, wy_send, wy_recv,
):
    users, rows, _ = cand.shape
    hist = kv.shape[1]
    inner = wq.shape[1]
    hidden_slots = wu.shape[0]
    g, s, u = lax.axis_index("grp"), lax.axis_index("seq"), lax.axis_index("usr")
    partner = u + 1 - 2 * lax.rem(u, 2)
    across = lax.rem(u + 2, 4)
    across_partner = lax.rem(partner + 2, 4)
    left, right = (g, s - 1, u), (g, s + 1, u)
    has_left, has_right = s > 0, s < seqs - 1

    first_owned = lax.rem(u, 2) * users
    owned = s - first_owned
    is_owner = jnp.logical_and(owned >= 0, owned < users)

    loads = {}
    for index, (name, source, target) in enumerate((
        ("cand", cand_hbm, cand), ("wq", wq_hbm, wq), ("kv", kv_hbm, kv), ("wg", wg_hbm, wg),
        ("tm", tm_hbm, tm.at[s]), ("wo", wo_hbm, wo), ("wu", wu_hbm, wu.at[u]), ("wd", wd_hbm, wd.at[u]),
    )):
        loads[name] = pltpu.make_async_copy(source, target, load_sem.at[index])

    for name in ("cand", "wq"):
        loads[name].start()

    barrier = pltpu.get_barrier_semaphore()
    peers = [(g, s, partner), (g, s, across), (1 - g, s, u)]
    peers += [(g, lax.rem(s + step, seqs), u) for step in range(1, seqs)]
    for peer in peers:
        pl.semaphore_signal(barrier, inc=1, device_id=peer, device_id_type=MESH)

    def remote(source, target, send, recv, device):
        return pltpu.make_async_remote_copy(
            src_ref=source, dst_ref=target, send_sem=send, recv_sem=recv,
            device_id=device, device_id_type=MESH,
        )

    weights = ((wu_hbm, wu), (wd_hbm, wd))

    def rows_of(piece, half):
        size = weights[piece // 2][1].shape[1] // 4
        return pl.ds(pl.multiple_of((half * 2 + piece % 2) * size, size), size)

    def piece_of(piece, slot, half):
        return weights[piece // 2][1].at[slot, rows_of(piece, half)]

    def to_partner_own(w, slot):
        return remote(weights[w][0], weights[w][1].at[slot], wo_send.at[w], wo_recv.at[w], (g, s, partner))

    def to_across(piece, slot):
        source = weights[piece // 2][0].at[rows_of(piece, g)]
        return remote(source, piece_of(piece, slot, g), wx_send.at[piece], wx_recv.at[piece], (g, s, across))

    def to_group(piece, half):
        part = piece_of(piece, across, half)
        return remote(part, part, wy_send.at[piece], wy_recv.at[piece], (1 - g, s, u))

    def to_partner_far(piece, slot, half, which):
        part = piece_of(piece, slot, half)
        return remote(part, part, wc_send.at[piece, which], wc_recv.at[piece, which], (g, s, partner))

    def across_arrived(piece):
        to_across(piece, across).wait_recv()
        to_group(piece, g).start()
        to_partner_far(piece, across, g, 0).start()

    def group_arrived(piece):
        to_group(piece, 1 - g).wait_recv()
        to_partner_far(piece, across, 1 - g, 1).start()

    def gather_copy(buf, send, recv, m, block, way):
        ref = buf.at[m, block]
        return remote(ref, ref, send.at[m, block, way], recv.at[m, block], (left, right)[way])

    def gather_step(buf, send, recv, m, step):
        @pl.when(s >= step)
        def _():
            block = s - step
            gather_copy(buf, send, recv, m, block, 1).wait_recv()

            @pl.when(has_right)
            def _():
                gather_copy(buf, send, recv, m, block, 1).start()

        @pl.when(s + step < seqs)
        def _():
            block = s + step
            gather_copy(buf, send, recv, m, block, 0).wait_recv()

            @pl.when(has_left)
            def _():
                gather_copy(buf, send, recv, m, block, 0).start()

    def gather_own(buf, send, recv, m):
        @pl.when(has_right)
        def _():
            gather_copy(buf, send, recv, m, s, 1).start()

        @pl.when(has_left)
        def _():
            gather_copy(buf, send, recv, m, s, 0).start()

    def gather_finish(buf, send, recv):
        for m in range(users):
            for block in range(seqs):
                @pl.when(jnp.logical_and(block <= s, has_right))
                def _():
                    gather_copy(buf, send, recv, m, block, 1).wait_send()

                @pl.when(jnp.logical_and(block >= s, has_left))
                def _():
                    gather_copy(buf, send, recv, m, block, 0).wait_send()

    loads["cand"].wait()
    loads["wq"].wait()
    for m in range(users):
        queries[m, s] = dot(cand[m], wq[...]).astype(BF16)
        if m == 0:
            pl.semaphore_wait(barrier, len(peers))
        gather_own(queries, q_send, q_recv, m)
    for piece in range(4):
        to_across(piece, u).start()
    for name in ("kv", "wg", "tm", "wo", "wu", "wd"):
        loads[name].start()
    for w in range(2):
        to_partner_own(w, u).start()

    loads["kv"].wait()
    for m in range(users):
        slots = s * hist + lax.broadcasted_iota(jnp.int32, (hist, 1), 0)
        visible = jnp.where(slots < len_ref[m], 1.0, 0.0)
        values[m] = (kv[m, :, inner:].astype(F32) * visible).astype(BF16)

    half_scale = 0.5 / math.sqrt(DH)

    def attend(m, block):
        for head in range(HEADS):
            cols = slice(head * DH, (head + 1) * DH)
            scores = lax.dot_general(
                queries[m, block, :, cols], kv[m, :, cols], (((1,), (1,)), ((), ())),
                preferred_element_type=F32,
            )
            weight = silu_of_double(scores * half_scale).astype(BF16)
            sums[m, block, :, cols] = dot(weight, values[m, :, cols])

    def partial_copy(m, block, way):
        return remote(
            outgoing.at[m, block], incoming.at[way, m, block],
            p_send.at[m, block], p_recv.at[way, m, block], (left, right)[way],
        )

    def pass_on(m, block, way, first):
        @pl.when(first)
        def _():
            outgoing[m, block] = sums[m, block].astype(BF16)

        @pl.when(jnp.logical_not(first))
        def _():
            partial_copy(m, block, way).wait_recv()
            outgoing[m, block] = (sums[m, block] + incoming[way, m, block].astype(F32)).astype(BF16)

        partial_copy(m, block, way).start()

    chip = lax.div(u, 2)
    quarter = rows // 4

    def quarter_rows(group, near):
        return pl.ds(pl.multiple_of((group * 2 + near) * quarter, quarter), quarter)

    def mix_copy(m):
        return remote(
            tm_hbm.at[quarter_rows(g, chip)], tm.at[s, quarter_rows(g, chip)],
            t_send.at[m], t_recv.at[s, 0], (g, first_owned + m, u),
        )

    def mix_share(block, which):
        part = tm.at[block, quarter_rows(g, 1 - chip if which == 3 else chip)]
        device = (g, s, across) if which == 1 else (1 - g, s, u)
        return remote(part, part, f_send.at[block, which], t_recv.at[block, which], device)

    def mix_arrived(block, which):
        part = tm.at[block, quarter_rows(1 - g if which > 1 else g, 1 - chip if which % 2 else chip)]
        remote(part, part, f_send.at[block, which], t_recv.at[block, which], (1 - g, s, u)).wait_recv()

    def for_far_blocks(do):
        for block in range(seqs):
            @pl.when(jnp.logical_and(is_owner, block != s))
            def _():
                do(block)

    def share_first(block):
        mix_arrived(block, 0)
        mix_share(block, 1).start()
        mix_share(block, 2).start()

    def share_second(block):
        mix_arrived(block, 1)
        mix_share(block, 3).start()

    def share_last(block):
        mix_arrived(block, 2)
        mix_arrived(block, 3)

    def share_sent(block):
        for which in (1, 2, 3):
            mix_share(block, which).wait_send()

    mirror = seqs - 1 - s
    def stage_of(step, m):
        if step < seqs:
            if step > 0:
                gather_step(queries, q_send, q_recv, m, step)

            @pl.when(s >= step)
            def _():
                attend(m, s - step)

            if step > 0:
                @pl.when(s + step < seqs)
                def _():
                    attend(m, s + step)

        owner = first_owned + m
        block = step - s

        @pl.when((owner > s) & (block >= 0) & (block < seqs))
        def _():
            pass_on(m, block, 1, s == 0)

        far = step - mirror

        @pl.when((owner < s) & (far >= 0) & (far < seqs))
        def _():
            pass_on(m, seqs - 1 - far, 0, mirror == 0)

    for step in range(2 * seqs - 2):
        for m in range(users):
            stage_of(step, m)

        if step == 0:
            loads["wg"].wait()
            for m in range(users):
                gates[m] = silu_of_double(dot(cand[m], wg[...]) * 0.5)
        if step == MIX_STEP:
            for m in range(users):
                @pl.when(first_owned + m != s)
                def _():
                    mix_copy(m).start()
        if step == SHARE_STEPS[0]:
            for_far_blocks(share_first)
        if step == SHARE_STEPS[1]:
            for_far_blocks(share_second)
        for piece in range(4):
            if step == ACROSS_STEPS[piece]:
                across_arrived(piece)
            if step == GROUP_STEPS[piece]:
                group_arrived(piece)

    def mixed_copy(block, m):
        return remote(
            mixed_out.at[block], mixed_in.at[m], m_send.at[block], m_recv.at[m], (g, block, u)
        )

    order = sorted(range(seqs), key=lambda block: min(block, seqs - 1 - block))
    loads["tm"].wait()
    @pl.when(is_owner)
    def _():
        for block in range(seqs):
            @pl.when(has_left)
            def _():
                partial_copy(owned, block, 1).wait_recv()
                sums[owned, block] = sums[owned, block] + incoming[1, owned, block].astype(F32)

            @pl.when(has_right)
            def _():
                partial_copy(owned, block, 0).wait_recv()
                sums[owned, block] = sums[owned, block] + incoming[0, owned, block].astype(F32)

            normed[block * rows:(block + 1) * rows] = layer_norm(sums[owned, block]).astype(BF16)
        for_far_blocks(share_last)
        for block in order:
            mixed = normed[block * rows:(block + 1) * rows].astype(F32) + dot(tm[block], normed[...])
            mixed_out[block] = mixed.astype(BF16)

            @pl.when(block != s)
            def _():
                mixed_copy(block, owned).start()

            @pl.when(block == s)
            def _():
                mixed_in[owned] = mixed.astype(BF16)

    for piece in range(4):
        if GROUP_STEPS[piece] >= 2 * seqs - 2:
            group_arrived(piece)
    loads["wo"].wait()
    ffn_ins = []
    for m in range(users):
        @pl.when(first_owned + m != s)
        def _():
            mixed_copy(s, m).wait_recv()

        gated = (mixed_in[m].astype(F32) * gates[m]).astype(BF16)
        state = cand[m].astype(F32) + dot(gated, wo[...])
        states[m * rows:(m + 1) * rows] = state
        ffn_ins.append(layer_norm(state).astype(BF16))
    ffn_in = jnp.concatenate(ffn_ins, axis=0)

    for w in range(2):
        loads[("wu", "wd")[w]].wait()
        to_partner_own(w, partner).wait_recv()
    for piece in range(4):
        to_partner_far(piece, across_partner, g, 0).wait_recv()
        to_partner_far(piece, across_partner, 1 - g, 1).wait_recv()
    total = states[...]
    for slot in range(hidden_slots):
        hidden = gelu_tanh(dot(ffn_in, wu[slot])).astype(BF16)
        total = total + dot(hidden, wd[slot])
    for m in range(users):
        out_ref[m] = total[m * rows:(m + 1) * rows].astype(BF16)

    gather_finish(queries, q_send, q_recv)
    for_far_blocks(share_sent)
    for m in range(users):
        @pl.when(first_owned + m != s)
        def _():
            mix_copy(m).wait_send()
            for block in range(seqs):
                partial_copy(m, block, 1).wait_send()

    @pl.when(is_owner)
    def _():
        for block in range(seqs):
            @pl.when(block != s)
            def _():
                mixed_copy(block, owned).wait_send()

    for w in range(2):
        to_partner_own(w, u).wait_send()
    for piece in range(4):
        to_across(piece, u).wait_send()
        to_group(piece, g).wait_send()
        to_partner_far(piece, across, g, 0).wait_send()
        to_partner_far(piece, across, 1 - g, 1).wait_send()


def fused(seqs, usrs, history_kv, candidates, lengths, w_query, w_gate, token_mix, w_out, w_up, w_down):
    users, hist, _ = history_kv.shape
    rows, width = candidates.shape[1:]
    inner = w_query.shape[1]
    depth = w_up.shape[1]
    dma = pltpu.SemaphoreType.DMA
    hbm = pl.BlockSpec(memory_space=pl.ANY)
    smem = pl.BlockSpec(memory_space=pltpu.SMEM)
    return pl.pallas_call(
        functools.partial(kernel, seqs),
        out_shape=jax.ShapeDtypeStruct(candidates.shape, BF16),
        in_specs=[hbm, hbm, smem, hbm, hbm, hbm, hbm, hbm, hbm],
        out_specs=pl.BlockSpec(memory_space=pltpu.VMEM),
        scratch_shapes=[
            pltpu.VMEM(history_kv.shape, BF16),
            pltpu.VMEM(candidates.shape, BF16),
            pltpu.VMEM(w_query.shape, BF16),
            pltpu.VMEM(w_gate.shape, BF16),
            pltpu.VMEM((seqs, *token_mix.shape), BF16),
            pltpu.VMEM(w_out.shape, BF16),
            pltpu.VMEM((usrs, width, depth), BF16),
            pltpu.VMEM((usrs, depth, width), BF16),
            pltpu.VMEM((users, hist, inner), BF16),
            pltpu.VMEM((users, seqs, rows, inner), BF16),
            pltpu.VMEM((users, seqs, rows, inner), F32),
            pltpu.VMEM((users, seqs, rows, inner), BF16),
            pltpu.VMEM((2, users, seqs, rows, inner), BF16),
            pltpu.VMEM((seqs * rows, inner), BF16),
            pltpu.VMEM((seqs, rows, inner), BF16),
            pltpu.VMEM((users, rows, inner), BF16),
            pltpu.VMEM((users, rows, inner), F32),
            pltpu.VMEM((users * rows, width), F32),
            dma((8,)),
            dma((users, seqs, 2)), dma((users, seqs)),
            dma((users, seqs)), dma((2, users, seqs)),
            dma((users,)), dma((seqs, 4)), dma((seqs, 4)), dma((seqs,)), dma((users,)),
            dma((2,)), dma((2,)), dma((4, 2)), dma((4, 2)),
            dma((4,)), dma((4,)), dma((4,)), dma((4,)),
        ],
        compiler_params=pltpu.CompilerParams(
            collective_id=0, has_side_effects=True, vmem_limit_bytes=56 * 1024 * 1024
        ),
        name="rank_layer",
    )(history_kv, candidates, lengths, w_query, w_gate, token_mix, w_out, w_up, w_down)


def shards(history_kv, candidates, lengths, w_query, w_gate, token_mix, w_out, w_up, w_down):
    user_count, hist_dev, _ = history_kv.shape
    inner = w_query.shape[1]
    half = hist_dev // 2
    scale = 1.0 / math.sqrt(DH)
    seq_index = lax.axis_index("seq")
    first_start = seq_index * hist_dev
    sections = ((history_kv[:, :half], first_start), (history_kv[:, half:], first_start + half))
    offsets = lax.iota(jnp.int32, half)
    queries = jnp.einsum(
        "ucd,de->uce", candidates, w_query, preferred_element_type=jnp.float32
    ).astype(jnp.bfloat16)
    piece = lax.all_gather(queries, "seq", axis=1, tiled=True)
    row_count = piece.shape[1]
    results = []
    for member in range(user_count):
        query_heads = piece[member].reshape(row_count, HEADS, DH)
        limit = lengths[member]
        summed = jnp.zeros((row_count, inner), jnp.float32)
        for section, section_start in sections:
            key_heads = section[member, :, :inner].reshape(half, HEADS, DH)
            value_heads = section[member, :, inner:].reshape(half, HEADS, DH)

            def compute(
                operand,
                key_heads=key_heads,
                value_heads=value_heads,
                section_start=section_start,
                query_heads=query_heads,
                limit=limit,
            ):
                scores = (
                    jnp.einsum(
                        "chd,thd->hct", query_heads, key_heads, preferred_element_type=jnp.float32
                    )
                    * scale
                )
                visible = section_start + offsets < limit
                weights = jnp.where(visible[None, None, :], jax.nn.silu(scores), 0.0).astype(
                    jnp.bfloat16
                )
                contrib = jnp.einsum(
                    "hct,thd->chd", weights, value_heads, preferred_element_type=jnp.float32
                )
                return contrib.reshape(row_count, inner)

            def skipped(operand):
                return jnp.zeros((row_count, inner), jnp.float32)

            summed = summed + lax.cond(section_start < limit, compute, skipped, 0)
        results.append(summed)
    partial_sums = jnp.stack(results)
    attended = lax.psum_scatter(partial_sums, "seq", scatter_dimension=1, tiled=True)
    normed = layer_norm(attended).astype(jnp.bfloat16)
    mixed = normed.astype(jnp.float32) + jnp.einsum(
        "cp,upe->uce",
        token_mix,
        lax.all_gather(normed, "seq", axis=1, tiled=True),
        preferred_element_type=jnp.float32,
    )
    gate_values = jax.nn.silu(
        jnp.einsum("ucd,de->uce", candidates, w_gate, preferred_element_type=jnp.float32)
    )
    gated = (mixed * gate_values).astype(jnp.bfloat16)
    state = candidates.astype(jnp.float32) + jnp.einsum(
        "uce,ed->ucd", gated, w_out, preferred_element_type=jnp.float32
    )
    ffn_in = layer_norm(state).astype(jnp.bfloat16)
    hidden = jax.nn.gelu(
        jnp.einsum(
            "ucd,df->ucf",
            lax.all_gather(ffn_in, "usr", axis=0, tiled=True),
            w_up,
            preferred_element_type=jnp.float32,
        )
    ).astype(jnp.bfloat16)
    ffn_terms = jnp.einsum("ucf,fd->ucd", hidden, w_down, preferred_element_type=jnp.float32)
    ffn_out = lax.psum_scatter(
        ffn_terms.astype(jnp.bfloat16), "usr", scatter_dimension=0, tiled=True
    ).astype(jnp.float32)
    return (state + ffn_out).astype(jnp.bfloat16)


def solution(mesh):
    sizes = dict(mesh.shape)
    seqs, usrs = sizes["seq"], sizes["usr"]
    def body(history_kv, candidates, *rest):
        operands = (history_kv, candidates, *rest)
        if sizes["grp"] == 2 and usrs == 4 and seqs == 2 * candidates.shape[0] and seqs >= 4:
            return fused(seqs, usrs, *operands)
        return shards(*operands)

    return jax.shard_map(
        body,
        mesh=mesh,
        in_specs=(
            P(("grp", "usr"), "seq", None),
            P(("grp", "usr"), "seq", None),
            P(("grp", "usr")),
            P(),
            P(),
            P("seq", None),
            P(),
            P(None, "usr"),
            P("usr", None),
        ),
        out_specs=P(("grp", "usr"), "seq", None),
        check_vma=False,
    )
```

profile of v0, /device:TPU:0, one launch (start us, length us, event | category | flops | bytes accessed | tf_op | source)
XLA Modules:
  0.0 44.8 jit_solution(16386342619432728989)
XLA Ops:
  0.0 43.0 %rank_layer.1 = bf16[2,128,768]{2,1,0:T(8,128)(2,1)} custom-call(bf16[2,512,768]{2,1,0:T(8,128)(2,1)} %kv_hbm.1, bf16[2,128,768]{2,1,0:T(8,128)(2,1)} %cand_hbm.1, s32[2]{0:T(128)} %len_ref.1, bf16[768,384]{1,0:T(8,128)(2,1)} %wq_hbm.1, bf16[768,384]{1,0:T(8,128)(2,1)} %wg_hbm.1, bf16[128,512]{1,0:T(8,128)(2,1)} %tm_hbm.1, bf16[384,768]{1,0:T(8,128)(2,1)} %wo_hbm.1, ...), custom_call_target="tpu_custom_call" | custom-call | tf_op jit(solution)/shard_map/rank_layer/pallas_call | solution.py:404
  43.0 1.8 %copy.11 = bf16[2,128,768]{2,1,0:T(8,128)(2,1)} copy(bf16[2,128,768]{2,1,0:T(8,128)(2,1)} %rank_layer.1) | data formatting | bytes 786432
where the time goes:
time: 45 us; the launch traced here: 44.8 us
  Pallas kernels  43 us (96%)
  local copies, waits for them, and re-layouts  1.77 us (4%)
    pallas_call x1, Pallas kernels, fused(): pl.pallas_call(functools.partial(kernel, seqs), out_shape=jax.ShapeDtypeS...  43 us
    unnamed x1, local copies, waits for them, and re-layouts  1.77 us

commit v1 on v0

--- a/solution.py
+++ b/solution.py
@@ -17,6 +17,7 @@
 GROUP_STEPS = (3, 4, 5, 6)
 MIX_STEP = 0
 SHARE_STEPS = (3, 4)
+COLUMNS = 256
 
 
 def layer_norm(values):
@@ -39,11 +40,11 @@
 
 def kernel(
     seqs,
-    kv_hbm, cand_hbm, len_ref, wq_hbm, wg_hbm, tm_hbm, wo_hbm, wu_hbm, wd_hbm,
+    kv_hbm, cand_hbm, len_hbm, wq_hbm, wg_hbm, tm_hbm, wo_hbm, wu_hbm, wd_hbm,
     out_ref,
     kv, cand, wq, wg, tm, wo, wu, wd,
     values, queries, sums, outgoing, incoming, normed, mixed_out, mixed_in, gates, states,
-    load_sem,
+    lens, load_sem,
     q_send, q_recv, p_send, p_recv, t_send, t_recv, f_send, m_send, m_recv,
     wo_send, wo_recv, wc_send, wc_recv, wx_send, wx_recv, wy_send, wy_recv,
 ):
@@ -65,11 +66,11 @@
     loads = {}
     for index, (name, source, target) in enumerate((
         ("cand", cand_hbm, cand), ("wq", wq_hbm, wq), ("kv", kv_hbm, kv), ("wg", wg_hbm, wg),
-        ("tm", tm_hbm, tm.at[s]), ("wo", wo_hbm, wo), ("wu", wu_hbm, wu.at[u]), ("wd", wd_hbm, wd.at[u]),
+        ("tm", tm_hbm, tm.at[s]), ("wo", wo_hbm, wo), ("wu", wu_hbm, wu.at[u]), ("wd", wd_hbm, wd.at[u]), ("lens", len_hbm, lens),
     )):
         loads[name] = pltpu.make_async_copy(source, target, load_sem.at[index])
 
-    for name in ("cand", "wq"):
+    for name in ("cand", "wq", "lens"):
         loads[name].start()
 
     barrier = pltpu.get_barrier_semaphore()
@@ -175,9 +176,10 @@
         to_partner_own(w, u).start()
 
     loads["kv"].wait()
+    loads["lens"].wait()
     for m in range(users):
         slots = s * hist + lax.broadcasted_iota(jnp.int32, (hist, 1), 0)
-        visible = jnp.where(slots < len_ref[m], 1.0, 0.0)
+        visible = jnp.where(slots < lens[m], 1.0, 0.0)
         values[m] = (kv[m, :, inner:].astype(F32) * visible).astype(BF16)
 
     half_scale = 0.5 / math.sqrt(DH)
@@ -361,12 +363,15 @@
     for piece in range(4):
         to_partner_far(piece, across_partner, g, 0).wait_recv()
         to_partner_far(piece, across_partner, 1 - g, 1).wait_recv()
-    total = states[...]
-    for slot in range(hidden_slots):
-        hidden = gelu_tanh(dot(ffn_in, wu[slot])).astype(BF16)
-        total = total + dot(hidden, wd[slot])
-    for m in range(users):
-        out_ref[m] = total[m * rows:(m + 1) * rows].astype(BF16)
+    width = cand.shape[2]
+    hidden = [gelu_tanh(dot(ffn_in, wu[slot])).astype(BF16) for slot in range(hidden_slots)]
+    for first in range(0, width, COLUMNS):
+        cols = slice(first, min(first + COLUMNS, width))
+        total = states[:, cols]
+        for slot in range(hidden_slots):
+            total = total + dot(hidden[slot], wd[slot, :, cols])
+        for m in range(users):
+            out_ref[m, :, cols] = total[m * rows:(m + 1) * rows].astype(BF16)
 
     gather_finish(queries, q_send, q_recv)
     for_far_blocks(share_sent)
@@ -399,12 +404,12 @@
     inner = w_query.shape[1]
     depth = w_up.shape[1]
     dma = pltpu.SemaphoreType.DMA
-    hbm = pl.BlockSpec(memory_space=pl.ANY)
-    smem = pl.BlockSpec(memory_space=pltpu.SMEM)
+    hbm = pl.BlockSpec(memory_space=pltpu.HBM)
+    operands = (history_kv, candidates, lengths, w_query, w_gate, token_mix, w_out, w_up, w_down)
     return pl.pallas_call(
         functools.partial(kernel, seqs),
         out_shape=jax.ShapeDtypeStruct(candidates.shape, BF16),
-        in_specs=[hbm, hbm, smem, hbm, hbm, hbm, hbm, hbm, hbm],
+        in_specs=[hbm] * len(operands),
         out_specs=pl.BlockSpec(memory_space=pltpu.VMEM),
         scratch_shapes=[
             pltpu.VMEM(history_kv.shape, BF16),
@@ -425,7 +430,8 @@
             pltpu.VMEM((users, rows, inner), BF16),
             pltpu.VMEM((users, rows, inner), F32),
             pltpu.VMEM((users * rows, width), F32),
-            dma((8,)),
+            pltpu.SMEM(lengths.shape, jnp.int32),
+            dma((9,)),
             dma((users, seqs, 2)), dma((users, seqs)),
             dma((users, seqs)), dma((2, users, seqs)),
             dma((users,)), dma((seqs, 4)), dma((seqs, 4)), dma((seqs,)), dma((users,)),
@@ -433,10 +439,10 @@
             dma((4,)), dma((4,)), dma((4,)), dma((4,)),
         ],
         compiler_params=pltpu.CompilerParams(
-            collective_id=0, has_side_effects=True, vmem_limit_bytes=56 * 1024 * 1024
+            collective_id=0, has_side_effects=True, vmem_limit_bytes=34 * 1024 * 1024
         ),
         name="rank_layer",
-    )(history_kv, candidates, lengths, w_query, w_gate, token_mix, w_out, w_up, w_down)
+    )(*(pltpu.with_memory_space_constraint(operand, pltpu.HBM) for operand in operands))
 
 
 def shards(history_kv, candidates, lengths, w_query, w_gate, token_mix, w_out, w_up, w_down):

time: 45 us -> 42.1 us (0.936)
  Pallas kernels: 43 us -> 41.2 us
  local copies, waits for them, and re-layouts: 1.77 us -> 0.75 us
    pallas_call x1, Pallas kernels: 43 us -> 41.2 us  [fused(): pl.pallas_call(functools.partial(kernel, seqs), out_shape=jax.ShapeDtypeS...]
    unnamed x1, local copies, waits for them, and re-layouts: 1.77 us -> 0.75 us
where the time goes in v1:
time: 42.1 us; the launch traced here: 42 us
  Pallas kernels  41.2 us (98%)
  local copies, waits for them, and re-layouts  0.75 us (2%)
    pallas_call x1, Pallas kernels, fused(): pl.pallas_call(functools.partial(kernel, seqs), out_shape=jax.ShapeDtypeS...  41.2 us

profile of v1, /device:TPU:0, one launch (start us, length us, event | category | flops | bytes accessed | tf_op | source)
XLA Modules:
  0.0 42.0 jit_solution(685873960735746593)
XLA Ops:
  0.0 41.2 %rank_layer.1 = bf16[2,128,768]{2,1,0:T(8,128)(2,1)S(1)} custom-call(bf16[2,512,768]{2,1,0:T(8,128)(2,1)} %kv_hbm.1, bf16[2,128,768]{2,1,0:T(8,128)(2,1)} %cand_hbm.1, s32[2]{0:T(128)} %len_hbm.1, bf16[768,384]{1,0:T(8,128)(2,1)} %wq_hbm.1, bf16[768,384]{1,0:T(8,128)(2,1)} %wg_hbm.1, bf16[128,512]{1,0:T(8,128)(2,1)} %tm_hbm.1, bf16[384,768]{1,0:T(8,128)(2,1)} %wo_hbm.1, ...), custom_call_target="tpu_custom_call" | custom-call | tf_op jit(solution)/shard_map/rank_layer/pallas_call | solution.py:409
  41.2 0.7 %copy.11 = bf16[2,128,768]{2,1,0:T(8,128)(2,1)} copy(bf16[2,128,768]{2,1,0:T(8,128)(2,1)S(1)} %rank_layer.1) | data formatting | bytes 786432

commit v2 on v1

v2 whole, which is shorter than its diff:
```python
import functools
import math

import jax
import jax.numpy as jnp
from jax import lax
from jax.experimental import pallas as pl
from jax.experimental.pallas import tpu as pltpu
from jax.sharding import PartitionSpec as P

HEADS = 3
DH = 128
F32 = jnp.float32
BF16 = jnp.bfloat16
MESH = pl.DeviceIdType.MESH
COLUMNS = 256
PIECES = 4
DEPTH = 2

(ATTEND, ARRIVED, PASS, SEND_SUM, COMPLETE, PIECE_ACROSS, PIECE_GROUP, SEND_MIX, PASS_MIX, PREMIX, MIX,
 SHARE_FIRST, SHARE_SECOND) = range(1, 14)
PLAN = (
    (
        (
            3001, 1000, 3102, 8000, 1100, 4101, 2110, 1110, 4111, 6000, 2010, 1010, 3101, 6001, 7000,
            6002, 7001, 6003, 12000, 7002, 6004, 7003, 2130, 1130, 6005, 4131, 2120, 1120, 13000, 4121,
            2020, 1020, 7004, 2030, 1030, 6006, 5030, 7005, 6007, 5000, 5020, 10000, 5010, 11000, 7006,
            7007,
        ),
        (
            3110, 3112, 3010, 1010, 4010, 1110, 3012, 2120, 1120, 6000, 2000, 3003, 1000, 4000, 6001,
            9000, 12000, 2130, 3130, 1130, 6002, 7000, 3120, 3002, 7001, 2020, 3020, 1020, 6003, 2100,
            1100, 13000, 7002, 2030, 3030, 1030, 6004, 4030, 7003, 6005, 4020, 5130, 5110, 6006, 7004,
            6007, 5120, 10000, 5100, 11000, 7005, 7006, 7007,
        ),
        (
            3121, 3123, 1120, 8000, 1020, 3023, 2130, 2110, 3131, 3113, 1130, 6000, 1110, 3021, 2100,
            3103, 1100, 4131, 6001, 2010, 3013, 1010, 6002, 7000, 6003, 7001, 2030, 3031, 1030, 4031,
            6004, 7002, 4121, 2000, 1000, 4021, 6005, 7003, 4111, 4000, 6006, 7004, 4101, 4010, 6007,
            7005, 7006, 7007,
        ),
        (
            3132, 1130, 4132, 8000, 1030, 4032, 6000, 3032, 2120, 1120, 4122, 6001, 2020, 1020, 4022,
            6002, 7000, 2110, 1110, 4112, 7001, 6003, 2000, 1000, 4002, 2100, 1100, 4102, 6004, 7002,
            2010, 1010, 4012, 7003, 6005, 7004, 6006, 7005, 6007, 7006, 7007,
        ),
    ),
    (
        (
            3001, 1000, 3102, 8000, 1100, 4101, 2010, 1010, 6000, 6001, 7000, 3101, 6002, 7001, 6003,
            7002, 6004, 12000, 2110, 1110, 6005, 4111, 7003, 2020, 1020, 2120, 1120, 4121, 7004, 6006,
            2130, 1130, 4131, 5020, 13000, 6007, 7005, 5010, 2030, 1030, 7006, 5030, 10000, 5000, 11000,
            7007,
        ),
        (
            3010, 1110, 3013, 1010, 4010, 3112, 2000, 1000, 4000, 6000, 3002, 3012, 6001, 2020, 1020,
            6002, 7000, 9000, 12000, 3110, 3020, 6003, 7001, 2100, 1100, 2120, 3120, 1120, 6004, 7002,
            2130, 3130, 1130, 13000, 4020, 6005, 7003, 2030, 3030, 1030, 5110, 6006, 7004, 4030, 6007,
            5130, 5120, 10000, 5100, 11000, 7005, 7006, 7007,
        ),
        (
            1020, 4021, 1120, 3021, 3023, 8000, 6000, 3123, 2110, 3113, 1110, 4111, 6001, 2100, 3103,
            1100, 7000, 6002, 3121, 2000, 3003, 1000, 6003, 2130, 3131, 1130, 7001, 4131, 2010, 1010,
            6004, 2030, 3031, 1030, 4031, 7002, 4010, 6005, 7003, 4121, 6006, 7004, 4101, 6007, 7005,
            4000, 7006, 7007,
        ),
        (
            1030, 8000, 4032, 1130, 4132, 3132, 6000, 3032, 2010, 1010, 4012, 2020, 1020, 6001, 4021,
            7000, 6002, 2120, 1120, 4122, 7001, 2110, 1110, 6003, 4111, 7002, 6004, 2100, 1100, 4102,
            7003, 2000, 1000, 6005, 4002, 7004, 6006, 7005, 6007, 7006, 7007,
        ),
    ),
)
QUERY_ORDER = (((0, 1), (0, 1), (0, 1), (0, 1)), ((0, 1), (0, 1), (0, 1), (0, 1)))
TAIL_ORDER = (((0, 1), (1, 0), (1, 0), (1, 0)), ((0, 1), (1, 0), (1, 0), (1, 0)))


def numbers_of(step):
    return step // 100 % 10, step // 10 % 10, step % 10


def steps_of(odd, k, kind):
    return [numbers_of(t) for t in PLAN[odd][k] if t // 1000 == kind]


def children(odd, k, m, b):
    return [j for j in range(len(PLAN[odd])) if (m, b, k) in steps_of(odd, j, SEND_SUM)]


def lanes_of(m):
    places = range(len(PLAN[0]))
    return max(len(children(odd, k, m, b)) for odd in range(2) for k in places for b in places)


def layer_norm(values):
    center = values - jnp.mean(values, axis=-1, keepdims=True)
    spread = jnp.mean(center * center, axis=-1, keepdims=True)
    return center * lax.rsqrt(spread + 1e-05)


def silu_of_double(half):
    return half + half * jnp.tanh(half)


def gelu_tanh(v):
    return 0.5 * v * (1.0 + jnp.tanh(math.sqrt(2.0 / math.pi) * (v + 0.044715 * (v * v * v))))


def dot(a, b):
    return jnp.dot(a, b, preferred_element_type=F32)


def kernel(
    seqs,
    kv_hbm, cand_hbm, len_hbm, wq_hbm, wg_hbm, tm_hbm, wo_hbm, wu_hbm, wd_hbm,
    out_ref,
    kv, cand, wq, wg, tm, wo, wu, wd,
    values, queries, sums, outgoing, incoming, normed, mixed_sum, mixed_out, mixed_in, gates, states,
    lens, load_sem,
    q_send, q_recv, p_send, p_recv, t_send, t_recv, f_send, m_send, m_recv,
    w_send, wo_recv, wx_recv, wy_recv, wc_recv, far,
):
    users, rows, width = cand.shape
    hist = kv.shape[1]
    inner = wq.shape[1]
    g, s, u = lax.axis_index("grp"), lax.axis_index("seq"), lax.axis_index("usr")
    odd = lax.rem(u, 2)
    partner = u + 1 - 2 * odd
    across = lax.rem(u + 2, 4)
    across_partner = lax.rem(partner + 2, 4)
    step = 1 - 2 * odd
    place = s + odd * (seqs - 1 - 2 * s)

    def user_of(m):
        return m + odd * (users - 1 - 2 * m)

    def block_of(b):
        return b + odd * (seqs - 1 - 2 * b)

    def at_place(b):
        return (g, block_of(b), u)

    variants = [(c, k) for c in range(2) for k in range(seqs)]
    variant = odd * seqs + place

    def pick(choices):
        if len(set(choices)) == 1:
            return choices[0]
        value = choices[-1]
        for v in range(len(choices) - 1):
            value = jnp.where(variant == v, choices[v], value)
        return value

    def by_variant(do):
        for v, (c, k) in enumerate(variants):
            @pl.when(variant == v)
            def _():
                do(c, k)

    loads = {}
    for index, (name, source, target) in enumerate((
        ("cand", cand_hbm, cand), ("wq", wq_hbm, wq), ("lens", len_hbm, lens), ("kv", kv_hbm, kv), ("wg", wg_hbm, wg),
        ("tm", tm_hbm, tm.at[s]), ("wo", wo_hbm, wo), ("wu", wu_hbm, wu.at[u]), ("wd", wd_hbm, wd.at[u]),
    )):
        loads[name] = pltpu.make_async_copy(source, target, load_sem.at[index])

    for name in ("cand", "wq", "lens"):
        loads[name].start()

    barrier = pltpu.get_barrier_semaphore()
    near = [(g, s, partner), (g, s, across), (1 - g, s, u)]
    for peer in near:
        pl.semaphore_signal(barrier, inc=1, device_id=peer, device_id_type=MESH)

    @pl.when(s > 0)
    def _():
        pl.semaphore_signal(barrier, inc=1, device_id=(g, s - 1, u), device_id_type=MESH)

    @pl.when(s < seqs - 1)
    def _():
        pl.semaphore_signal(barrier, inc=1, device_id=(g, s + 1, u), device_id_type=MESH)

    def remote(source, target, send, recv, device):
        return pltpu.make_async_remote_copy(
            src_ref=source, dst_ref=target, send_sem=send, recv_sem=recv,
            device_id=device, device_id_type=MESH,
        )

    def drain(ref, sem):
        pltpu.make_async_copy(ref, ref, sem).wait()

    weights = ((wu_hbm, wu), (wd_hbm, wd))

    def rows_of(piece, half):
        size = weights[piece // PIECES][1].shape[1] // (2 * PIECES)
        return pl.ds(pl.multiple_of((half * PIECES + piece % PIECES) * size, size), size)

    def piece_of(piece, slot, half):
        return weights[piece // PIECES][1].at[slot, rows_of(piece, half)]

    def to_partner_own(w):
        return remote(weights[w][0], weights[w][1].at[u], w_send.at[w], wo_recv.at[w], (g, s, partner))

    def to_across(piece, slot):
        w = piece // PIECES
        source = weights[w][0].at[rows_of(piece, g)]
        return remote(source, piece_of(piece, slot, g), w_send.at[w], wx_recv.at[piece], (g, s, across))

    def to_group(piece, half):
        part = piece_of(piece, across, half)
        return remote(part, part, w_send.at[piece // PIECES], wy_recv.at[piece], (1 - g, s, u))

    def to_partner_far(piece, half):
        part = piece_of(piece, across, half)
        w = piece // PIECES
        return remote(part, part, w_send.at[w], wc_recv.at[w], (g, s, partner))

    def across_arrived(piece):
        to_across(piece, across).wait_recv()
        if piece + DEPTH < 2 * PIECES:
            to_across(piece + DEPTH, u).start()
        to_group(piece, g).start()
        to_partner_far(piece, g).start()

    def group_arrived(piece):
        to_group(piece, 1 - g).wait_recv()
        to_partner_far(piece, 1 - g).start()

    def query_copy(m, b, to):
        ref = queries.at[m, b]
        return remote(ref, ref, q_send, q_recv.at[m, b], at_place(to))

    def early(c, k):
        kinds = [t // 1000 for t in PLAN[c][k]]
        ahead = [t for t in PLAN[c][k][:kinds.index(ATTEND)] if t // 1000 == PASS]
        return [t for t in ahead if numbers_of(t)[:2] == (QUERY_ORDER[c][k][0], k) and abs(t % 10 - k) == 1]

    def pass_queries(m, b, to):
        query_copy(m, b, to).start()

    def send_early(c, k):
        for t in early(c, k):
            pass_queries(*numbers_of(t))

    orders = [QUERY_ORDER[c][k] for c, k in variants]
    first, second = pick([o[0] for o in orders]), pick([o[1] for o in orders])
    loads["cand"].wait()
    loads["wq"].wait()
    loads["kv"].start()
    queries[first, place] = dot(cand[user_of(first)], wq[...]).astype(BF16)
    neighbours = (s > 0).astype(jnp.int32) + (s < seqs - 1).astype(jnp.int32)
    pl.semaphore_wait(barrier, len(near) + neighbours)
    by_variant(send_early)
    for piece in range(DEPTH):
        to_across(piece, u).start()
    for way in (-1, 1):
        @pl.when((s + way >= 0) & (s + way < seqs))
        def _():
            pl.semaphore_signal(far, inc=1, device_id=(g, s + way, u), device_id_type=MESH)

    queries[second, place] = dot(cand[user_of(second)], wq[...]).astype(BF16)
    for w in range(2):
        to_partner_own(w).start()
    for name in ("wg", "tm", "wo", "wu", "wd"):
        loads[name].start()

    loads["lens"].wait()
    loads["kv"].wait()
    for m in range(users):
        slots = s * hist + lax.broadcasted_iota(jnp.int32, (hist, 1), 0)
        visible = jnp.where(slots < lens[m], 1.0, 0.0)
        values[m] = (kv[m, :, inner:].astype(F32) * visible).astype(BF16)

    half_scale = 0.5 / math.sqrt(DH)

    def attend(m, b):
        user = user_of(m)
        for head in range(HEADS):
            cols = slice(head * DH, (head + 1) * DH)
            scores = lax.dot_general(
                queries[m, b, :, cols], kv[user, :, cols], (((1,), (1,)), ((), ())),
                preferred_element_type=F32,
            )
            weight = silu_of_double(scores * half_scale).astype(BF16)
            sums[m, b, :, cols] = dot(weight, values[user, :, cols])

    lane_start = [sum(lanes_of(j) for j in range(m)) for m in range(users)]

    def sum_copy(c, source, m, b, to):
        lane = lane_start[m] + children(c, to, m, b).index(source)
        return remote(
            outgoing.at[m, b], incoming.at[lane * seqs + b], p_send, p_recv.at[lane, b], at_place(to)
        )

    def gather_sum(c, k, m, b):
        total = sums[m, b]
        for child in children(c, k, m, b):
            copy = sum_copy(c, child, m, b, k)
            copy.wait_recv()
            lane = lane_start[m] + children(c, k, m, b).index(child)
            total = total + incoming[lane * seqs + b].astype(F32)
        return total

    def send_sum(c, k, m, b, to):
        outgoing[m, b] = gather_sum(c, k, m, b).astype(BF16)
        sum_copy(c, k, m, b, to).start()

    def sum_complete(c, k, m, b):
        first_row = pl.multiple_of(block_of(b) * rows, rows)
        normed[pl.ds(first_row, rows)] = layer_norm(gather_sum(c, k, m, b)).astype(BF16)

    chip = lax.div(u, 2)
    quarter = rows // 4

    def quarter_rows(group, near_chip):
        return pl.ds(pl.multiple_of((group * 2 + near_chip) * quarter, quarter), quarter)

    def send_mix(k):
        mine = quarter_rows(g, chip)
        remote(tm_hbm.at[mine], tm.at[s, mine], t_send, t_recv.at[0], at_place(1)).start()

    def mix_arrived(turn):
        drain(tm.at[pl.ds(0, seqs - 1), pl.ds(0, quarter)], t_recv.at[turn])

    def pass_mix():
        mix_arrived(0)
        part = tm.at[pl.ds(1 - odd, seqs - 1), quarter_rows(g, chip)]
        remote(part, part, t_send, t_recv.at[0], at_place(0)).start()

    def mix_share(k, near_chip, turn):
        for b in range(seqs):
            if b != k:
                part = tm.at[block_of(b), quarter_rows(g, near_chip)]
                device = (g, s, across) if turn == 1 else (1 - g, s, u)
                remote(part, part, f_send, t_recv.at[turn], device).start()

    def share_first(k):
        if k == 0:
            mix_arrived(0)
        mix_share(k, chip, 1)
        mix_share(k, chip, 2)

    def share_second(k):
        mix_arrived(1)
        mix_share(k, 1 - chip, 3)

    def mixed_copy(to, m):
        return remote(mixed_out.at[to], mixed_in.at[m], m_send, m_recv.at[m], at_place(to))

    def premix(c, k):
        last_row = pl.multiple_of(block_of(steps_of(c, k, COMPLETE)[-1][1]) * rows, rows)
        normed[pl.ds(last_row, rows)] = jnp.zeros((rows, inner), BF16)
        mix_arrived(2)
        mix_arrived(3)
        for b in range(seqs):
            first_row = pl.multiple_of(block_of(b) * rows, rows)
            mixed_sum[b] = normed[pl.ds(first_row, rows)].astype(F32) + dot(tm[block_of(b)], normed[...])

    def mix(c, k):
        last = steps_of(c, k, COMPLETE)[-1][1]
        last_rows = pl.ds(pl.multiple_of(block_of(last) * rows, rows), rows)
        late = normed[last_rows]
        for b in sorted(range(seqs), key=lambda b: -abs(b - k)):
            mixed = mixed_sum[b] + dot(tm[block_of(b), :, last_rows], late)
            if b == last:
                mixed = mixed + late.astype(F32)
            if b == k:
                mixed_in[k] = mixed.astype(BF16)
            else:
                mixed_out[b] = mixed.astype(BF16)
                mixed_copy(b, k).start()

    def act(c, k, step):
        kind, (m, b, to) = step // 1000, numbers_of(step)
        if kind == PASS:
            pass_queries(m, b, to)
        elif kind == ARRIVED:
            query_copy(m, b, k).wait_recv()
        elif kind == SEND_SUM:
            send_sum(c, k, m, b, to)
        elif kind == COMPLETE:
            sum_complete(c, k, m, b)
        elif kind == PIECE_ACROSS:
            across_arrived(step % 100)
        elif kind == PIECE_GROUP:
            group_arrived(step % 100)
        elif kind == SEND_MIX:
            send_mix(k)
        elif kind == PASS_MIX:
            pass_mix()
        elif kind == PREMIX:
            premix(c, k)
        elif kind == MIX:
            mix(c, k)
        elif kind == SHARE_FIRST:
            share_first(k)
        elif kind == SHARE_SECOND:
            share_second(k)

    def run(c, k, steps):
        for step in steps:
            act(c, k, step)

    parts = []
    for c, k in variants:
        parts.append([[]])
        skipped = early(c, k)
        for t in PLAN[c][k]:
            if t not in skipped:
                parts[-1][-1].append(t)
            if t // 1000 == ATTEND:
                parts[-1].append([])
    for index in range(users * seqs):
        by_variant(lambda c, k: run(c, k, parts[c * seqs + k][index][:-1]))
        chosen = [numbers_of(part[index][-1]) for part in parts]
        attend(pick([n[0] for n in chosen]), pick([n[1] for n in chosen]))
        if index == 0:
            pl.semaphore_wait(far, neighbours)
            loads["wg"].wait()
            loads["tm"].wait()
            for m in range(users):
                gates[m] = silu_of_double(dot(cand[user_of(m)], wg[...]) * 0.5)
    by_variant(lambda c, k: run(c, k, parts[c * seqs + k][-1]))

    loads["wo"].wait()
    slots = (u, partner, across, across_partner)
    for index in range(users):
        m = pick([TAIL_ORDER[c][k][index] for c, k in variants])

        @pl.when(place != m)
        def _():
            mixed_copy(place, m).wait_recv()

        user = user_of(m)
        gated = (mixed_in[m].astype(F32) * gates[m]).astype(BF16)
        state = cand[user].astype(F32) + dot(gated, wo[...])
        states[...] = state
        ffn_in = layer_norm(state).astype(BF16)
        if index == 0:
            loads["wu"].wait()
            remote(wu_hbm, wu.at[partner], w_send.at[0], wo_recv.at[0], (g, s, partner)).wait_recv()
            drain(wu.at[across_partner], wc_recv.at[0])
        hidden = [gelu_tanh(dot(ffn_in, wu[slot])).astype(BF16) for slot in slots]
        if index == 0:
            loads["wd"].wait()
            remote(wd_hbm, wd.at[partner], w_send.at[1], wo_recv.at[1], (g, s, partner)).wait_recv()
            drain(wd.at[across_partner], wc_recv.at[1])
        for start in range(0, width, COLUMNS):
            cols = slice(start, min(start + COLUMNS, width))
            total = states[:, cols]
            for h, slot in zip(hidden, slots):
                total = total + dot(h, wd[slot, :, cols])
            out_ref[user, :, cols] = total.astype(BF16)

    def finish(c, k):
        def blocks(kind):
            return incoming.at[pl.ds(0, len(steps_of(c, k, kind)))]

        drain(blocks(PASS), q_send)
        drain(blocks(SEND_SUM), p_send)
        drain(tm.at[pl.ds(0, seqs - 1 if k == 1 else 1), pl.ds(0, quarter)], t_send)
        if k < users:
            drain(tm.at[pl.ds(0, seqs - 1), pl.ds(0, 3 * quarter)], f_send)
            drain(incoming.at[pl.ds(0, seqs - 1)], m_send)

    by_variant(finish)
    drain(wu.at[pl.ds(0, 3)], w_send.at[0])
    drain(wd.at[pl.ds(0, 3)], w_send.at[1])


def fused(seqs, usrs, history_kv, candidates, lengths, w_query, w_gate, token_mix, w_out, w_up, w_down):
    users, hist, _ = history_kv.shape
    rows, width = candidates.shape[1:]
    inner = w_query.shape[1]
    depth = w_up.shape[1]
    dma = pltpu.SemaphoreType.DMA
    hbm = pl.BlockSpec(memory_space=pltpu.HBM)
    lanes = sum(lanes_of(m) for m in range(users))
    operands = (history_kv, candidates, lengths, w_query, w_gate, token_mix, w_out, w_up, w_down)
    return pl.pallas_call(
        functools.partial(kernel, seqs),
        out_shape=jax.ShapeDtypeStruct(candidates.shape, BF16),
        in_specs=[hbm] * len(operands),
        out_specs=pl.BlockSpec(memory_space=pltpu.VMEM),
        scratch_shapes=[
            pltpu.VMEM(history_kv.shape, BF16),
            pltpu.VMEM(candidates.shape, BF16),
            pltpu.VMEM(w_query.shape, BF16),
            pltpu.VMEM(w_gate.shape, BF16),
            pltpu.VMEM((seqs, *token_mix.shape), BF16),
            pltpu.VMEM(w_out.shape, BF16),
            pltpu.VMEM((usrs, width, depth), BF16),
            pltpu.VMEM((usrs, depth, width), BF16),
            pltpu.VMEM((users, hist, inner), BF16),
            pltpu.VMEM((users, seqs, rows, inner), BF16),
            pltpu.VMEM((users, seqs, rows, inner), F32),
            pltpu.VMEM((users, seqs, rows, inner), BF16),
            pltpu.VMEM((lanes * seqs, rows, inner), BF16),
            pltpu.VMEM((seqs * rows, inner), BF16),
            pltpu.VMEM((seqs, rows, inner), F32),
            pltpu.VMEM((seqs, rows, inner), BF16),
            pltpu.VMEM((users, rows, inner), BF16),
            pltpu.VMEM((users, rows, inner), F32),
            pltpu.VMEM((rows, width), F32),
            pltpu.SMEM(lengths.shape, jnp.int32),
            dma((9,)),
            dma, dma((users, seqs)), dma, dma((lanes, seqs)),
            dma, dma((4,)), dma, dma, dma((users,)),
            dma((2,)), dma((2,)), dma((2 * PIECES,)), dma((2 * PIECES,)), dma((2,)),
            pltpu.SemaphoreType.REGULAR,
        ],
        compiler_params=pltpu.CompilerParams(
            collective_id=0, has_side_effects=True, vmem_limit_bytes=34 * 1024 * 1024
        ),
        name="rank_layer",
    )(*(pltpu.with_memory_space_constraint(operand, pltpu.HBM) for operand in operands))


def shards(history_kv, candidates, lengths, w_query, w_gate, token_mix, w_out, w_up, w_down):
    user_count, hist_dev, _ = history_kv.shape
    inner = w_query.shape[1]
    half = hist_dev // 2
    scale = 1.0 / math.sqrt(DH)
    seq_index = lax.axis_index("seq")
    first_start = seq_index * hist_dev
    sections = ((history_kv[:, :half], first_start), (history_kv[:, half:], first_start + half))
    offsets = lax.iota(jnp.int32, half)
    queries = jnp.einsum(
        "ucd,de->uce", candidates, w_query, preferred_element_type=jnp.float32
    ).astype(jnp.bfloat16)
    piece = lax.all_gather(queries, "seq", axis=1, tiled=True)
    row_count = piece.shape[1]
    results = []
    for member in range(user_count):
        query_heads = piece[member].reshape(row_count, HEADS, DH)
        limit = lengths[member]
        summed = jnp.zeros((row_count, inner), jnp.float32)
        for section, section_start in sections:
            key_heads = section[member, :, :inner].reshape(half, HEADS, DH)
            value_heads = section[member, :, inner:].reshape(half, HEADS, DH)

            def compute(
                operand,
                key_heads=key_heads,
                value_heads=value_heads,
                section_start=section_start,
                query_heads=query_heads,
                limit=limit,
            ):
                scores = (
                    jnp.einsum(
                        "chd,thd->hct", query_heads, key_heads, preferred_element_type=jnp.float32
                    )
                    * scale
                )
                visible = section_start + offsets < limit
                weights = jnp.where(visible[None, None, :], jax.nn.silu(scores), 0.0).astype(
                    jnp.bfloat16
                )
                contrib = jnp.einsum(
                    "hct,thd->chd", weights, value_heads, preferred_element_type=jnp.float32
                )
                return contrib.reshape(row_count, inner)

            def skipped(operand):
                return jnp.zeros((row_count, inner), jnp.float32)

            summed = summed + lax.cond(section_start < limit, compute, skipped, 0)
        results.append(summed)
    partial_sums = jnp.stack(results)
    attended = lax.psum_scatter(partial_sums, "seq", scatter_dimension=1, tiled=True)
    normed = layer_norm(attended).astype(jnp.bfloat16)
    mixed = normed.astype(jnp.float32) + jnp.einsum(
        "cp,upe->uce",
        token_mix,
        lax.all_gather(normed, "seq", axis=1, tiled=True),
        preferred_element_type=jnp.float32,
    )
    gate_values = jax.nn.silu(
        jnp.einsum("ucd,de->uce", candidates, w_gate, preferred_element_type=jnp.float32)
    )
    gated = (mixed * gate_values).astype(jnp.bfloat16)
    state = candidates.astype(jnp.float32) + jnp.einsum(
        "uce,ed->ucd", gated, w_out, preferred_element_type=jnp.float32
    )
    ffn_in = layer_norm(state).astype(jnp.bfloat16)
    hidden = jax.nn.gelu(
        jnp.einsum(
            "ucd,df->ucf",
            lax.all_gather(ffn_in, "usr", axis=0, tiled=True),
            w_up,
            preferred_element_type=jnp.float32,
        )
    ).astype(jnp.bfloat16)
    ffn_terms = jnp.einsum("ucf,fd->ucd", hidden, w_down, preferred_element_type=jnp.float32)
    ffn_out = lax.psum_scatter(
        ffn_terms.astype(jnp.bfloat16), "usr", scatter_dimension=0, tiled=True
    ).astype(jnp.float32)
    return (state + ffn_out).astype(jnp.bfloat16)


def solution(mesh):
    sizes = dict(mesh.shape)
    seqs, usrs = sizes["seq"], sizes["usr"]
    def body(history_kv, candidates, *rest):
        operands = (history_kv, candidates, *rest)
        fits = sizes["grp"] == 2 and usrs == 4 and seqs == len(PLAN[0])
        if fits and candidates.shape[0] == len(QUERY_ORDER[0][0]):
            return fused(seqs, usrs, *operands)
        return shards(*operands)

    return jax.shard_map(
        body,
        mesh=mesh,
        in_specs=(
            P(("grp", "usr"), "seq", None),
            P(("grp", "usr"), "seq", None),
            P(("grp", "usr")),
            P(),
            P(),
            P("seq", None),
            P(),
            P(None, "usr"),
            P("usr", None),
        ),
        out_specs=P(("grp", "usr"), "seq", None),
        check_vma=False,
    )
```

time: 42.1 us -> 39.9 us (0.948)
  the two profiles are of different devices: /device:TPU:0 before, /device:TPU:15 now
where the time goes in v2:
time: 39.9 us; the launch traced here: 39.8 us
  Pallas kernels  39 us (98%)
  local copies, waits for them, and re-layouts  0.75 us (2%)
    pallas_call x1, Pallas kernels, fused(): pl.pallas_call(functools.partial(kernel, seqs), out_shape=jax.ShapeDtypeS...  39 us

profile of v2, /device:TPU:15, one launch (start us, length us, event | category | flops | bytes accessed | tf_op | source)
XLA Modules:
  0.0 39.8 jit_solution(1890346188551905703)
XLA Ops:
  0.0 39.0 %rank_layer.1 = bf16[2,128,768]{2,1,0:T(8,128)(2,1)S(1)} custom-call(bf16[2,512,768]{2,1,0:T(8,128)(2,1)} %kv_hbm.1, bf16[2,128,768]{2,1,0:T(8,128)(2,1)} %cand_hbm.1, s32[2]{0:T(128)} %len_hbm.1, bf16[768,384]{1,0:T(8,128)(2,1)} %wq_hbm.1, bf16[768,384]{1,0:T(8,128)(2,1)} %wg_hbm.1, bf16[128,512]{1,0:T(8,128)(2,1)} %tm_hbm.1, bf16[384,768]{1,0:T(8,128)(2,1)} %wo_hbm.1, ...), custom_call_target="tpu_custom_call" | custom-call | tf_op jit(solution)/shard_map/rank_layer/pallas_call | solution.py:480
  39.0 0.7 %copy.11 = bf16[2,128,768]{2,1,0:T(8,128)(2,1)} copy(bf16[2,128,768]{2,1,0:T(8,128)(2,1)S(1)} %rank_layer.1) | data formatting | bytes 786432

commit v3 on v2

--- a/solution.py
+++ b/solution.py
@@ -15,64 +15,63 @@
 MESH = pl.DeviceIdType.MESH
 COLUMNS = 256
 PIECES = 4
-DEPTH = 2
+DEPTH = 4
+LATE_LOADS = 6
 
 (ATTEND, ARRIVED, PASS, SEND_SUM, COMPLETE, PIECE_ACROSS, PIECE_GROUP, SEND_MIX, PASS_MIX, PREMIX, MIX,
  SHARE_FIRST, SHARE_SECOND) = range(1, 14)
 PLAN = (
     (
         (
-            3001, 1000, 3102, 8000, 1100, 4101, 2110, 1110, 4111, 6000, 2010, 1010, 3101, 6001, 7000,
-            6002, 7001, 6003, 12000, 7002, 6004, 7003, 2130, 1130, 6005, 4131, 2120, 1120, 13000, 4121,
-            2020, 1020, 7004, 2030, 1030, 6006, 5030, 7005, 6007, 5000, 5020, 10000, 5010, 11000, 7006,
-            7007,
-        ),
-        (
-            3110, 3112, 3010, 1010, 4010, 1110, 3012, 2120, 1120, 6000, 2000, 3003, 1000, 4000, 6001,
-            9000, 12000, 2130, 3130, 1130, 6002, 7000, 3120, 3002, 7001, 2020, 3020, 1020, 6003, 2100,
-            1100, 13000, 7002, 2030, 3030, 1030, 6004, 4030, 7003, 6005, 4020, 5130, 5110, 6006, 7004,
-            6007, 5120, 10000, 5100, 11000, 7005, 7006, 7007,
-        ),
-        (
-            3121, 3123, 1120, 8000, 1020, 3023, 2130, 2110, 3131, 3113, 1130, 6000, 1110, 3021, 2100,
-            3103, 1100, 4131, 6001, 2010, 3013, 1010, 6002, 7000, 6003, 7001, 2030, 3031, 1030, 4031,
-            6004, 7002, 4121, 2000, 1000, 4021, 6005, 7003, 4111, 4000, 6006, 7004, 4101, 4010, 6007,
-            7005, 7006, 7007,
-        ),
-        (
-            3132, 1130, 4132, 8000, 1030, 4032, 6000, 3032, 2120, 1120, 4122, 6001, 2020, 1020, 4022,
-            6002, 7000, 2110, 1110, 4112, 7001, 6003, 2000, 1000, 4002, 2100, 1100, 4102, 6004, 7002,
-            2010, 1010, 4012, 7003, 6005, 7004, 6006, 7005, 6007, 7006, 7007,
+            3101, 3001, 1000, 8000, 1100, 4101, 6000, 2010, 1010, 6001, 2110, 1110, 4111, 2020, 7000,
+            1020, 6002, 12000, 7001, 6003, 2120, 1120, 4121, 6004, 7002, 2130, 1130, 4131, 13000, 7003,
+            6005, 5020, 7004, 6006, 2030, 1030, 6007, 5030, 5010, 10000, 5000, 11000, 7005, 7006, 7007,
+        ),
+        (
+            3012, 1010, 3010, 1110, 3110, 3112, 2020, 3020, 1020, 2100, 4020, 1100, 2000, 3002, 6000,
+            3102, 1000, 4000, 2120, 1120, 9000, 12000, 6001, 3120, 2130, 3130, 1130, 6002, 7000, 13000,
+            6003, 7001, 6004, 2030, 7002, 3030, 1030, 4030, 5120, 6005, 4010, 5130, 6006, 7003, 5110,
+            6007, 10000, 5100, 11000, 7004, 7005, 7006, 7007,
+        ),
+        (
+            3021, 3121, 3123, 1020, 8000, 1120, 4121, 2010, 1010, 3013, 6000, 2130, 3131, 1130, 3023,
+            6001, 4131, 2110, 3113, 1110, 6002, 7000, 2000, 1000, 3003, 2100, 3103, 1100, 6003, 4101,
+            7001, 2030, 3031, 1030, 4031, 6004, 7002, 4011, 4020, 6005, 7003, 4111, 6006, 7004, 4000,
+            6007, 7005, 7006, 7007,
+        ),
+        (
+            3132, 1130, 8000, 4132, 1030, 4032, 3032, 6000, 2120, 1120, 4121, 6001, 7000, 6002, 2010,
+            1010, 4012, 7001, 2020, 1020, 4022, 6003, 7002, 2110, 1110, 4112, 6004, 2000, 1000, 4002,
+            7003, 6005, 2100, 1100, 4101, 7004, 6006, 7005, 6007, 7006, 7007,
         ),
     ),
     (
         (
-            3001, 1000, 3102, 8000, 1100, 4101, 2010, 1010, 6000, 6001, 7000, 3101, 6002, 7001, 6003,
-            7002, 6004, 12000, 2110, 1110, 6005, 4111, 7003, 2020, 1020, 2120, 1120, 4121, 7004, 6006,
-            2130, 1130, 4131, 5020, 13000, 6007, 7005, 5010, 2030, 1030, 7006, 5030, 10000, 5000, 11000,
-            7007,
-        ),
-        (
-            3010, 1110, 3013, 1010, 4010, 3112, 2000, 1000, 4000, 6000, 3002, 3012, 6001, 2020, 1020,
-            6002, 7000, 9000, 12000, 3110, 3020, 6003, 7001, 2100, 1100, 2120, 3120, 1120, 6004, 7002,
-            2130, 3130, 1130, 13000, 4020, 6005, 7003, 2030, 3030, 1030, 5110, 6006, 7004, 4030, 6007,
-            5130, 5120, 10000, 5100, 11000, 7005, 7006, 7007,
-        ),
-        (
-            1020, 4021, 1120, 3021, 3023, 8000, 6000, 3123, 2110, 3113, 1110, 4111, 6001, 2100, 3103,
-            1100, 7000, 6002, 3121, 2000, 3003, 1000, 6003, 2130, 3131, 1130, 7001, 4131, 2010, 1010,
-            6004, 2030, 3031, 1030, 4031, 7002, 4010, 6005, 7003, 4121, 6006, 7004, 4101, 6007, 7005,
-            4000, 7006, 7007,
-        ),
-        (
-            1030, 8000, 4032, 1130, 4132, 3132, 6000, 3032, 2010, 1010, 4012, 2020, 1020, 6001, 4021,
-            7000, 6002, 2120, 1120, 4122, 7001, 2110, 1110, 6003, 4111, 7002, 6004, 2100, 1100, 4102,
-            7003, 2000, 1000, 6005, 4002, 7004, 6006, 7005, 6007, 7006, 7007,
+            3101, 1000, 8000, 1100, 4101, 3001, 6000, 2010, 1010, 6001, 2020, 1020, 7000, 6002, 7001,
+            12000, 6003, 7002, 2110, 1110, 4111, 6004, 13000, 2120, 1120, 4121, 7003, 6005, 2130, 1130,
+            4131, 7004, 6006, 2030, 1030, 5030, 6007, 5020, 7005, 5000, 10000, 5010, 11000, 7006, 7007,
+        ),
+        (
+            3112, 1010, 4010, 1110, 3010, 2020, 3020, 1020, 6000, 2100, 1100, 3102, 3012, 6001, 9000,
+            12000, 3110, 6002, 7000, 2000, 3002, 1000, 6003, 7001, 2120, 3120, 1120, 2130, 3130, 1130,
+            13000, 6004, 7002, 2030, 3030, 1030, 6005, 7003, 4030, 4020, 6006, 4000, 5120, 5110, 6007,
+            7004, 5100, 10000, 5130, 11000, 7005, 7006, 7007,
+        ),
+        (
+            3023, 3123, 3021, 1120, 4121, 8000, 1020, 2110, 1110, 6000, 6001, 6002, 7000, 3121, 3113,
+            2130, 3131, 1130, 4131, 2100, 3103, 1100, 6003, 7001, 2030, 3031, 1030, 4031, 2010, 3013,
+            1010, 6004, 7002, 4021, 2000, 3003, 1000, 4001, 6005, 7003, 4111, 6006, 7004, 4101, 6007,
+            7005, 4010, 7006, 7007,
+        ),
+        (
+            1030, 8000, 1130, 4132, 3132, 4032, 2020, 1020, 3032, 4022, 2120, 1120, 4121, 6000, 6001,
+            7000, 6002, 7001, 6003, 2110, 1110, 4112, 6004, 7002, 2100, 1100, 6005, 4102, 7003, 2010,
+            1010, 6006, 4012, 7004, 2000, 1000, 4000, 7005, 6007, 7006, 7007,
         ),
     ),
 )
 QUERY_ORDER = (((0, 1), (0, 1), (0, 1), (0, 1)), ((0, 1), (0, 1), (0, 1), (0, 1)))
-TAIL_ORDER = (((0, 1), (1, 0), (1, 0), (1, 0)), ((0, 1), (1, 0), (1, 0), (1, 0)))
+TAIL_ORDER = (((0, 1), (1, 0), (0, 1), (1, 0)), ((0, 1), (1, 0), (0, 1), (1, 0)))
 
 
 def numbers_of(step):
@@ -103,7 +102,9 @@
 
 
 def gelu_tanh(v):
-    return 0.5 * v * (1.0 + jnp.tanh(math.sqrt(2.0 / math.pi) * (v + 0.044715 * (v * v * v))))
+    slope = math.sqrt(2.0 / math.pi)
+    half = 0.5 * v
+    return half + half * jnp.tanh(v * (slope + (0.044715 * slope) * (v * v)))
 
 
 def dot(a, b):
@@ -259,17 +260,8 @@
             pl.semaphore_signal(far, inc=1, device_id=(g, s + way, u), device_id_type=MESH)
 
     queries[second, place] = dot(cand[user_of(second)], wq[...]).astype(BF16)
-    for w in range(2):
-        to_partner_own(w).start()
-    for name in ("wg", "tm", "wo", "wu", "wd"):
+    for name in ("wg", "tm"):
         loads[name].start()
-
-    loads["lens"].wait()
-    loads["kv"].wait()
-    for m in range(users):
-        slots = s * hist + lax.broadcasted_iota(jnp.int32, (hist, 1), 0)
-        visible = jnp.where(slots < lens[m], 1.0, 0.0)
-        values[m] = (kv[m, :, inner:].astype(F32) * visible).astype(BF16)
 
     half_scale = 0.5 / math.sqrt(DH)
 
@@ -412,6 +404,13 @@
                 parts[-1].append([])
     for index in range(users * seqs):
         by_variant(lambda c, k: run(c, k, parts[c * seqs + k][index][:-1]))
+        if index == 0:
+            loads["lens"].wait()
+            loads["kv"].wait()
+            for m in range(users):
+                slots = s * hist + lax.broadcasted_iota(jnp.int32, (hist, 1), 0)
+                visible = jnp.where(slots < lens[m], 1.0, 0.0)
+                values[m] = (kv[m, :, inner:].astype(F32) * visible).astype(BF16)
         chosen = [numbers_of(part[index][-1]) for part in parts]
         attend(pick([n[0] for n in chosen]), pick([n[1] for n in chosen]))
         if index == 0:
@@ -420,6 +419,11 @@
             loads["tm"].wait()
             for m in range(users):
                 gates[m] = silu_of_double(dot(cand[user_of(m)], wg[...]) * 0.5)
+        if index == LATE_LOADS:
+            for w in range(2):
+                to_partner_own(w).start()
+            for name in ("wo", "wu", "wd"):
+                loads[name].start()
     by_variant(lambda c, k: run(c, k, parts[c * seqs + k][-1]))
 
     loads["wo"].wait()

time: 39.9 us -> 38.1 us (0.955)
  the two profiles are of different devices: /device:TPU:15 before, /device:TPU:0 now
where the time goes in v3:
time: 38.1 us; the launch traced here: 37.7 us
  Pallas kernels  37 us (97%)
  local copies, waits for them, and re-layouts  0.75 us (2%)
    pallas_call x1, Pallas kernels, fused(): pl.pallas_call(functools.partial(kernel, seqs), out_shape=jax.ShapeDtypeS...  37 us

profile of v3, /device:TPU:0, one launch (start us, length us, event | category | flops | bytes accessed | tf_op | source)
XLA Modules:
  0.0 37.7 jit_solution(2859953579813526236)
XLA Ops:
  0.0 37.0 %rank_layer.1 = bf16[2,128,768]{2,1,0:T(8,128)(2,1)S(1)} custom-call(bf16[2,512,768]{2,1,0:T(8,128)(2,1)} %kv_hbm.1, bf16[2,128,768]{2,1,0:T(8,128)(2,1)} %cand_hbm.1, s32[2]{0:T(128)} %len_hbm.1, bf16[768,384]{1,0:T(8,128)(2,1)} %wq_hbm.1, bf16[768,384]{1,0:T(8,128)(2,1)} %wg_hbm.1, bf16[128,512]{1,0:T(8,128)(2,1)} %tm_hbm.1, bf16[384,768]{1,0:T(8,128)(2,1)} %wo_hbm.1, ...), custom_call_target="tpu_custom_call" | custom-call | tf_op jit(solution)/shard_map/rank_layer/pallas_call | solution.py:484
  37.0 0.7 %copy.11 = bf16[2,128,768]{2,1,0:T(8,128)(2,1)} copy(bf16[2,128,768]{2,1,0:T(8,128)(2,1)S(1)} %rank_layer.1) | data formatting | bytes 786432

commit v4 on v3

--- a/solution.py
+++ b/solution.py
@@ -15,7 +15,7 @@
 MESH = pl.DeviceIdType.MESH
 COLUMNS = 256
 PIECES = 4
-DEPTH = 4
+DEPTH = 3
 LATE_LOADS = 6
 
 (ATTEND, ARRIVED, PASS, SEND_SUM, COMPLETE, PIECE_ACROSS, PIECE_GROUP, SEND_MIX, PASS_MIX, PREMIX, MIX,
@@ -23,50 +23,50 @@
 PLAN = (
     (
         (
-            3101, 3001, 1000, 8000, 1100, 4101, 6000, 2010, 1010, 6001, 2110, 1110, 4111, 2020, 7000,
-            1020, 6002, 12000, 7001, 6003, 2120, 1120, 4121, 6004, 7002, 2130, 1130, 4131, 13000, 7003,
-            6005, 5020, 7004, 6006, 2030, 1030, 6007, 5030, 5010, 10000, 5000, 11000, 7005, 7006, 7007,
-        ),
-        (
-            3012, 1010, 3010, 1110, 3110, 3112, 2020, 3020, 1020, 2100, 4020, 1100, 2000, 3002, 6000,
-            3102, 1000, 4000, 2120, 1120, 9000, 12000, 6001, 3120, 2130, 3130, 1130, 6002, 7000, 13000,
-            6003, 7001, 6004, 2030, 7002, 3030, 1030, 4030, 5120, 6005, 4010, 5130, 6006, 7003, 5110,
-            6007, 10000, 5100, 11000, 7004, 7005, 7006, 7007,
-        ),
-        (
-            3021, 3121, 3123, 1020, 8000, 1120, 4121, 2010, 1010, 3013, 6000, 2130, 3131, 1130, 3023,
-            6001, 4131, 2110, 3113, 1110, 6002, 7000, 2000, 1000, 3003, 2100, 3103, 1100, 6003, 4101,
-            7001, 2030, 3031, 1030, 4031, 6004, 7002, 4011, 4020, 6005, 7003, 4111, 6006, 7004, 4000,
+            3001, 3101, 1100, 4101, 8000, 1000, 2010, 1010, 6000, 2110, 1110, 4111, 6001, 6002, 7000,
+            6003, 7001, 12000, 6004, 7002, 2130, 1130, 6005, 4131, 7003, 2020, 1020, 2120, 1120, 4121,
+            13000, 5020, 6006, 7004, 2030, 1030, 5030, 6007, 7005, 5000, 10000, 5010, 11000, 7006, 7007,
+        ),
+        (
+            3010, 3012, 3110, 3112, 1110, 1010, 2000, 3002, 1000, 4000, 6000, 2100, 3102, 1100, 6001,
+            9000, 12000, 6002, 7000, 2130, 3130, 1130, 6003, 7001, 2020, 3020, 1020, 2120, 3120, 1120,
+            13000, 4020, 6004, 7002, 2030, 3030, 1030, 4030, 6005, 7003, 4010, 6006, 5130, 5110, 6007,
+            7004, 5120, 10000, 5100, 11000, 7005, 7006, 7007,
+        ),
+        (
+            3123, 3023, 1120, 8000, 1020, 4021, 2010, 3013, 1010, 6000, 2130, 1130, 3131, 2110, 3113,
+            1110, 3021, 3121, 6001, 4131, 6002, 7000, 2000, 3003, 1000, 2100, 3103, 1100, 6003, 7001,
+            2030, 3031, 1030, 4031, 6004, 7002, 4121, 6005, 7003, 4011, 4111, 6006, 7004, 4000, 4101,
             6007, 7005, 7006, 7007,
         ),
         (
-            3132, 1130, 8000, 4132, 1030, 4032, 3032, 6000, 2120, 1120, 4121, 6001, 7000, 6002, 2010,
-            1010, 4012, 7001, 2020, 1020, 4022, 6003, 7002, 2110, 1110, 4112, 6004, 2000, 1000, 4002,
-            7003, 6005, 2100, 1100, 4101, 7004, 6006, 7005, 6007, 7006, 7007,
+            3132, 1030, 8000, 1130, 4132, 4032, 2120, 1120, 3032, 4122, 6000, 2020, 1020, 4021, 6001,
+            2010, 1010, 4012, 7000, 6002, 2110, 1110, 6003, 7001, 4112, 2000, 1000, 4002, 7002, 6004,
+            2100, 1100, 4102, 7003, 6005, 7004, 6006, 7005, 6007, 7006, 7007,
         ),
     ),
     (
         (
-            3101, 1000, 8000, 1100, 4101, 3001, 6000, 2010, 1010, 6001, 2020, 1020, 7000, 6002, 7001,
-            12000, 6003, 7002, 2110, 1110, 4111, 6004, 13000, 2120, 1120, 4121, 7003, 6005, 2130, 1130,
-            4131, 7004, 6006, 2030, 1030, 5030, 6007, 5020, 7005, 5000, 10000, 5010, 11000, 7006, 7007,
-        ),
-        (
-            3112, 1010, 4010, 1110, 3010, 2020, 3020, 1020, 6000, 2100, 1100, 3102, 3012, 6001, 9000,
-            12000, 3110, 6002, 7000, 2000, 3002, 1000, 6003, 7001, 2120, 3120, 1120, 2130, 3130, 1130,
-            13000, 6004, 7002, 2030, 3030, 1030, 6005, 7003, 4030, 4020, 6006, 4000, 5120, 5110, 6007,
-            7004, 5100, 10000, 5130, 11000, 7005, 7006, 7007,
-        ),
-        (
-            3023, 3123, 3021, 1120, 4121, 8000, 1020, 2110, 1110, 6000, 6001, 6002, 7000, 3121, 3113,
-            2130, 3131, 1130, 4131, 2100, 3103, 1100, 6003, 7001, 2030, 3031, 1030, 4031, 2010, 3013,
-            1010, 6004, 7002, 4021, 2000, 3003, 1000, 4001, 6005, 7003, 4111, 6006, 7004, 4101, 6007,
-            7005, 4010, 7006, 7007,
-        ),
-        (
-            1030, 8000, 1130, 4132, 3132, 4032, 2020, 1020, 3032, 4022, 2120, 1120, 4121, 6000, 6001,
-            7000, 6002, 7001, 6003, 2110, 1110, 4112, 6004, 7002, 2100, 1100, 6005, 4102, 7003, 2010,
-            1010, 6006, 4012, 7004, 2000, 1000, 4000, 7005, 6007, 7006, 7007,
+            3001, 3101, 1000, 8000, 1100, 4101, 6000, 2110, 1110, 6001, 4111, 7000, 6002, 12000, 6003,
+            7001, 7002, 6004, 13000, 2010, 1010, 2130, 1130, 4131, 7003, 6005, 2120, 1120, 4121, 2020,
+            1020, 7004, 6006, 5020, 2030, 1030, 6007, 5030, 5010, 7005, 10000, 5000, 11000, 7006, 7007,
+        ),
+        (
+            3112, 3012, 1010, 4010, 1110, 3110, 2000, 3002, 1000, 6000, 4000, 2120, 1120, 2100, 3102,
+            1100, 6001, 9000, 12000, 6002, 7000, 2130, 1130, 3010, 3130, 3120, 6003, 7001, 2020, 3020,
+            1020, 13000, 6004, 7002, 4020, 2030, 3030, 1030, 6005, 7003, 4030, 5100, 5130, 6006, 5110,
+            10000, 5120, 11000, 6007, 7004, 7005, 7006, 7007,
+        ),
+        (
+            3023, 3121, 1020, 8000, 1120, 4121, 3123, 2110, 3113, 1110, 2010, 3013, 1010, 6000, 6001,
+            2130, 3131, 1130, 2000, 3003, 3021, 1000, 4131, 6002, 7000, 2100, 3103, 1100, 4101, 6003,
+            7001, 4021, 2030, 3031, 1030, 4031, 7002, 6004, 4111, 6005, 7003, 4010, 4000, 6006, 7004,
+            6007, 7005, 7006, 7007,
+        ),
+        (
+            1130, 8000, 3132, 4132, 1030, 4032, 2020, 1020, 6000, 4022, 3032, 2120, 1120, 4121, 6001,
+            2110, 1110, 4112, 6002, 7000, 2010, 1010, 4012, 2000, 1000, 6003, 7001, 4002, 2100, 1100,
+            7002, 6004, 4101, 6005, 7003, 6006, 7004, 6007, 7005, 7006, 7007,
         ),
     ),
 )

time: 38.1 us -> 37.6 us (0.987)
  no operation moved by 1% of the time
where the time goes in v4:
time: 37.6 us; the launch traced here: 37.5 us
  Pallas kernels  36.7 us (98%)
  local copies, waits for them, and re-layouts  0.75 us (2%)
    pallas_call x1, Pallas kernels, fused(): pl.pallas_call(functools.partial(kernel, seqs), out_shape=jax.ShapeDtypeS...  36.7 us

profile of v4, /device:TPU:0, one launch (start us, length us, event | category | flops | bytes accessed | tf_op | source)
XLA Modules:
  0.0 37.5 jit_solution(18168460260068427431)
XLA Ops:
  0.0 36.7 %rank_layer.1 = bf16[2,128,768]{2,1,0:T(8,128)(2,1)S(1)} custom-call(bf16[2,512,768]{2,1,0:T(8,128)(2,1)} %kv_hbm.1, bf16[2,128,768]{2,1,0:T(8,128)(2,1)} %cand_hbm.1, s32[2]{0:T(128)} %len_hbm.1, bf16[768,384]{1,0:T(8,128)(2,1)} %wq_hbm.1, bf16[768,384]{1,0:T(8,128)(2,1)} %wg_hbm.1, bf16[128,512]{1,0:T(8,128)(2,1)} %tm_hbm.1, bf16[384,768]{1,0:T(8,128)(2,1)} %wo_hbm.1, ...), custom_call_target="tpu_custom_call" | custom-call | tf_op jit(solution)/shard_map/rank_layer/pallas_call | solution.py:484
  36.7 0.7 %copy.11 = bf16[2,128,768]{2,1,0:T(8,128)(2,1)} copy(bf16[2,128,768]{2,1,0:T(8,128)(2,1)S(1)} %rank_layer.1) | data formatting | bytes 786432
